TPU v7x, 32 devices: a whole 2x2x4 slice. The times are simulated.
32 devices in a mesh: wide: 16 (over z, y, x), narrow: 2 (over core).
Axes of the slice: x: 2, y: 2, z: 4, core: 2. Of those that a mesh axis runs over, the one named last changes fastest.
Arguments:
- amplitudes: bfloat16 [32768, 1024], P('wide', 'narrow'), may hold values from -6 to 6
- pair_mask: int32 [256, 8], P('wide', 'narrow'), may hold values 0 or 1
- integrals: bfloat16 [1024, 4096], P('wide', 'narrow'), may hold values from -0.1875 to 0.1875
Outputs:
- ladder: bfloat16 [32768, 4096], P('wide', 'narrow')
All inputs are finite; a program needn't handle non-finite values. No bound on the sum of `pair_mask` on one device may be relied on, other than what follows from the above.
Results may differ from a plain program's by a relative error of at most 0.001.
Values may be sent and summed in bfloat16 or wider, within the bound.
No kernel may reach another device: no remote copies, remote signals or barrier semaphores. Data moves between devices by JAX's collectives and lax.ppermute only.
A program may use at most 64 MiB of HBM per device.

v0:
```python
import jax
import jax.numpy as jnp
from jax import lax
from jax.sharding import PartitionSpec as P

VB = 128


def shards(amplitudes, pair_mask, integrals):
    tiles = jnp.repeat(jnp.repeat(pair_mask, VB, axis=0), VB, axis=1)
    masked = amplitudes * tiles.astype(jnp.bfloat16)
    whole_rows = lax.all_gather(masked, "narrow", axis=1, tiled=True)
    result = jnp.dot(
        whole_rows,
        lax.all_gather(integrals, "wide", axis=0, tiled=True),
        preferred_element_type=jnp.float32,
    )
    return result.astype(jnp.bfloat16)


def solution(mesh):
    in_specs = (P("wide", "narrow"), P("wide", "narrow"), P("wide", "narrow"))
    out_specs = P("wide", "narrow")
    return jax.shard_map(shards, mesh=mesh, in_specs=in_specs, out_specs=out_specs, check_vma=False)
```

profile of v0, /device:TPU:0, one launch (start us, length us, event | category | flops | bytes accessed | tf_op | source)
XLA Modules:
  0.0 131.8 jit_solution(240691390158238495)
XLA Ops:
  6.5 0.0 copy-start
  6.5 0.0 all-gather.3.cloned.1.call-start
  6.5 0.8 convert_element_type.14
  7.4 0.1 copy.4
  7.5 0.1 broadcast_in_dim.6
  7.5 5.8 %broadcast_in_dim.7 = bf16[2048,4,128]{2,1,0:T(4,128)(2,1)S(1)} broadcast(bf16[2048,4]{1,0:T(8,128)(2,1)S(1)} %bitcast.7), dimensions={0,1} | broadcast | bytes 2113536 | tf_op jit(solution)/shard_map/broadcast_in_dim | solution.py:10
  13.3 0.0 copy-done
  13.3 1.6 %bitcast_multiply_fusion = bf16[2048,512]{1,0:T(8,128)(2,1)} fusion(bf16[2048,512]{1,0:T(8,128)(2,1)S(1)} %copy-done, bf16[256,8,4,128]{3,2,1,0:T(4,128)(2,1)S(1)} %bitcast.6), kind=kLoop, calls=%fused_computation.1 | loop fusion | flops 1048576 | bytes 6291456 | tf_op jit(solution)/shard_map/mul | solution.py:11
  14.9 0.0 all-gather.3.cloned.1.call-update
  15.0 0.0 all-gather.5.cloned.1.call-start
  15.0 0.7 all-gather.5.cloned.1.call-update
  15.7 15.8 %all-gather.3.cloned.1.call-done = bf16[2048,1024]{1,0:T(8,128)(2,1)} async-done(((bf16[2048,512]{1,0:T(8,128)(2,1)}), bf16[2048,1024]{1,0:T(8,128)(2,1)}) %all-gather.3.cloned.1.call-update) | async-done | bytes 4194320 | tf_op jit(solution)/shard_map/all_gather | solution.py:12
  31.5 79.6 %all-gather.5.cloned.1.call-done = bf16[1024,2048]{1,0:T(8,128)(2,1)} async-done(((bf16[64,2048]{1,0:T(8,128)(2,1)}), bf16[1024,2048]{1,0:T(8,128)(2,1)}) %all-gather.5.cloned.1.call-update) | async-done | bytes 4194320 | tf_op jit(solution)/shard_map/all_gather | solution.py:15
  111.1 13.9 %convolution_convert_fusion = bf16[2048,2048]{1,0:T(8,128)(2,1)} fusion(bf16[2048,1024]{1,0:T(8,128)(2,1)} %all-gather.3.cloned.1.call-done, bf16[1024,2048]{1,0:T(8,128)(2,1)} %all-gather.5.cloned.1.call-done), kind=kOutput, calls=%fused_computation | convolution fusion | flops 8594128896 | bytes 16777216 | tf_op jit(solution)/shard_map/dot_general | solution.py:13
Async XLA Ops:
  6.5 6.8 %copy-start = (bf16[2048,512]{1,0:T(8,128)(2,1)S(1)}, bf16[2048,512]{1,0:T(8,128)(2,1)}, u32[]{:S(2)}) copy-start(bf16[2048,512]{1,0:T(8,128)(2,1)} %param.3) | copy-start | bytes 6291460
  6.5 25.0 %all-gather.3.cloned.1.call-start = ((), (), s32[]{:S(2)}) async-start(), calls=%async_computation | async-start | bytes 6291456 | tf_op jit(solution)/shard_map/all_gather | solution.py:12
  15.0 96.1 %all-gather.5.cloned.1.call-start = ((), (), s32[]{:S(2)}) async-start(), calls=%async_computation.1 | async-start | bytes 4456448 | tf_op jit(solution)/shard_map/all_gather | solution.py:15
Sparse Core Ops, SparseCore 0:
  15.1 16.3 all-gather.2
  34.3 76.7 all-gather.4
where the time goes:
time: 132 us
  waiting for transfers between devices  96.1 us (73%)
  matrix products  13.9 us (11%)
  between operations  13.4 us (10%)
  local copies, waits for them, and re-layouts  5.96 us (5%)
  other arithmetic  2.43 us (2%)
    all_gather x1, waiting for transfers between devices, shards(): lax.all_gather(integrals, 'wide', axis=0, tiled=True)  79.6 us
    all_gather x1, waiting for transfers between devices, shards(): whole_rows = lax.all_gather(masked, 'narrow', axis=1, tiled=True)  15.8 us
    dot_general x1, matrix products, shards(): jnp.dot(whole_rows, lax.all_gather(integrals, 'wide', axis=0, tiled=True)...  13.9 us
    broadcast_in_dim x2, local copies, waits for them, and re-layouts, shards(): tiles = jnp.repeat(jnp.repeat(pair_mask, VB, axis=0), VB, axis=1)  5.86 us
  transfers between devices with their start and end apart: 2, of which 2 were waited for; matrix products, arithmetic and copies ran while one was open for 0% of the time, Pallas kernels for 0%

commit v1 on v0

v1 whole, which is shorter than its diff:
```python
import functools

import jax
import jax.numpy as jnp
from jax import lax
from jax.experimental import pallas as pl
from jax.experimental.pallas import tpu as pltpu
from jax.sharding import PartitionSpec as P


AXES = ("wide", "narrow")
TILE = 512
SPANS = 4


def placed(round_, chunk, per_part):
    at = (lax.axis_index("wide") // 4) ^ round_
    owner = (at // per_part) ^ lax.axis_index("narrow")
    return owner, lax.rem(at, per_part) * chunk


def panel_kernel(rounds, chunk, parts, *refs):
    masks, panels = refs[:parts], refs[parts : 2 * parts]
    out_ref, held, sems = refs[2 * parts :]
    rows, across = panels[0].shape
    high = rows // masks[0].shape[1]
    broad = across // masks[0].shape[0]
    span = rows // sems.shape[1]

    def copy(j, s):
        at = pl.ds(s * span, span)
        return pltpu.make_async_copy(panels[j].at[at], held.at[j, at], sems.at[j, s])

    for s in range(sems.shape[1]):
        for j in range(parts):
            copy(j, s).start()
    for s in range(sems.shape[1]):
        for j in range(parts):
            copy(j, s).wait()
        for r in range(rounds):
            owner, column = placed(r, chunk, across // chunk)
            for j in range(parts):

                @pl.when(owner == j)
                def _():
                    for m in range(span // high):
                        row = s * (span // high) + m
                        for k in range(chunk // broad):
                            keep = masks[j][column // broad + k, row]
                            start = pl.multiple_of(column + k * broad, broad)
                            tile = held[j, row * high : (row + 1) * high, pl.ds(start, broad)]
                            out_ref[
                                r, row * high : (row + 1) * high, k * broad : (k + 1) * broad
                            ] = tile * keep.astype(jnp.float32).astype(tile.dtype)


def make_panel(masks, panels, rounds, chunk):
    rows, across = panels[0].shape
    parts = len(panels)
    moved = parts * rows * across * 2
    return pl.pallas_call(
        functools.partial(panel_kernel, rounds, chunk, parts),
        out_shape=jax.ShapeDtypeStruct((rounds, rows, chunk), panels[0].dtype),
        in_specs=[pl.BlockSpec(memory_space=pltpu.SMEM)] * parts
        + [pl.BlockSpec(memory_space=pltpu.HBM)] * parts,
        out_specs=pl.BlockSpec(memory_space=pltpu.VMEM),
        scratch_shapes=[
            pltpu.VMEM((parts, rows, across), panels[0].dtype),
            pltpu.SemaphoreType.DMA((parts, SPANS)),
        ],
        compiler_params=pltpu.CompilerParams(vmem_limit_bytes=12 * 2**20),
        cost_estimate=pl.CostEstimate(flops=0, bytes_accessed=moved, transcendentals=0),
        name="panel",
    )(*masks, pltpu.with_memory_space_constraint(panels[0], pltpu.HBM), *panels[1:])


def product_kernel(rounds, first, last, *refs):
    refs = list(refs)
    panel = refs.pop(0)
    pieces = [[refs.pop(0) for _ in range(4)] for _ in rounds]
    before = None if first else refs.pop(0)
    out_ref, b_buf = refs
    depth = pieces[0][0].shape[0]
    chunk = 4 * depth

    @pl.when(pl.program_id(0) == 0)
    def _():
        place = lax.rem(lax.axis_index("wide"), 4)
        flip = 1 + lax.rem(lax.axis_index("narrow"), 2)
        spots = (place, place ^ flip, place ^ (3 - flip), place ^ 3)
        for i in range(len(rounds)):
            for spot, piece in zip(spots, pieces[i]):
                at = pl.multiple_of(i * chunk + spot * depth, depth)
                b_buf[pl.ds(at, depth)] = piece[...]

    at = pl.ds(pl.multiple_of(pl.program_id(0) * TILE, TILE), TILE)
    a = jnp.concatenate([panel[r, at] for r in rounds], axis=1)
    for n in range(0, b_buf.shape[1], 256):
        total = jnp.dot(a, b_buf[:, n : n + 256], preferred_element_type=jnp.float32)
        if before is not None:
            total += before[at, n : n + 256]
        if last:
            out_ref[:, n : n + 256] = total.astype(out_ref.dtype)
        else:
            out_ref[at, n : n + 256] = total


def product(panel, pieces, before, rounds, last):
    _, rows, chunk = panel.shape
    columns = pieces[0][0].shape[1]
    whole = pl.BlockSpec(memory_space=pltpu.VMEM)
    flat = [x for four in pieces for x in four]
    flops = 2 * rows * chunk * len(rounds) * columns
    first = before is None
    return pl.pallas_call(
        functools.partial(product_kernel, rounds, first, last),
        out_shape=jax.ShapeDtypeStruct(
            (rows, columns), panel.dtype if last else jnp.float32
        ),
        grid=(rows // TILE,),
        in_specs=[whole] * (1 + len(flat) + (not first)),
        out_specs=pl.BlockSpec((TILE, columns), lambda i: (i, 0)) if last else whole,
        scratch_shapes=[pltpu.VMEM((len(rounds) * chunk, columns), panel.dtype)],
        input_output_aliases={} if first or last else {1 + len(flat): 0},
        compiler_params=pltpu.CompilerParams(vmem_limit_bytes=16 * 2**20),
        cost_estimate=pl.CostEstimate(
            flops=flops, bytes_accessed=rows * columns * 2, transcendentals=0
        ),
    )(panel, *flat, *([] if first else [before]))


def shards(sizes, amplitudes, pair_mask, integrals):
    wide, narrow = sizes
    layers = wide // 4

    def exchange(value, flip):
        pairs = [
            (w * narrow + c, (w ^ flip(c)) * narrow + c)
            for w in range(wide)
            for c in range(narrow)
        ]
        return lax.ppermute(value, AXES, pairs)

    def swap(value, flip):
        return lax.ppermute(value, "narrow", [(c, c ^ flip) for c in range(narrow)])

    panels = [amplitudes] + [swap(amplitudes, j) for j in range(1, narrow)]
    turned = pair_mask.T
    masks = [turned] + [swap(turned, j) for j in range(1, narrow)]
    panel = make_panel(masks, panels, layers, 4 * integrals.shape[0])
    total = None
    for r in range(layers):
        own = exchange(integrals, lambda c: 4 * r) if r else integrals
        near = exchange(own, lambda c: 1 + c % 2)
        side = exchange(own, lambda c: 2 - c % 2)
        far = exchange(near, lambda c: 2 - c % 2)
        total = product(panel, [(own, near, side, far)], total, [r], r == layers - 1)
    return total


def solution(mesh):
    sizes = (mesh.shape["wide"], mesh.shape["narrow"])
    specs = P("wide", "narrow")
    return jax.shard_map(
        functools.partial(shards, sizes), mesh=mesh, in_specs=(specs,) * 3, out_specs=specs, check_vma=False
    )
```

time: 132 us -> 59.2 us (0.45)
  the two profiles are of different devices: /device:TPU:0 before, /device:TPU:16 now
where the time goes in v1:
time: 59.2 us; the launch traced here: 59 us
  waiting for transfers between devices  21.2 us (36%)
  Pallas kernels  19.7 us (33%)
  starting transfers between devices  17.4 us (29%)
  local copies, waits for them, and re-layouts  0.68 us (1%)
    ppermute x15, waiting for transfers between devices, exchange(): return lax.ppermute(value, AXES, pairs)  21.2 us
    ppermute x15, starting transfers between devices, exchange(): return lax.ppermute(value, AXES, pairs)  17.4 us
    pallas_call x4, Pallas kernels, product(): pl.pallas_call(functools.partial(product_kernel, rounds, first, last), ou...  16.9 us
    pallas_call x1, Pallas kernels, make_panel(): pl.pallas_call(functools.partial(panel_kernel, rounds, chunk, parts), out...  2.83 us
  transfers between devices with their start and end apart: 17, of which 4 were waited for; matrix products, arithmetic and copies ran while one was open for 0% of the time, Pallas kernels for 25%

profile of v1, /device:TPU:16, one launch (start us, length us, event | category | flops | bytes accessed | tf_op | source)
XLA Modules:
  0.0 59.0 jit_solution(8471898906379013050)
XLA Ops:
  0.0 0.0 copy-start
  0.0 0.0 collective-permute-start.1
  0.0 1.6 %collective-permute-start.14 = (bf16[64,2048]{1,0:T(8,128)(2,1)}, bf16[64,2048]{1,0:T(8,128)(2,1)S(1)}, u32[]{:S(2)}, u32[]{:S(2)}) collective-permute-start(bf16[64,2048]{1,0:T(8,128)(2,1)} %refs_1_.1), channel_id=1, source_target_pairs={{0,2},{1,5},{2,0},{3,7},{4,6},{5,1},{6,4},{7,3},{8,10},{9,13},{10,... | collective-permute-start | bytes 786440 | tf_op jit(solution)/shard_map/ppermute | solution.py:142
  1.6 1.6 %collective-permute-start.10 = (bf16[64,2048]{1,0:T(8,128)(2,1)}, bf16[64,2048]{1,0:T(8,128)(2,1)S(1)}, u32[]{:S(2)}, u32[]{:S(2)}) collective-permute-start(bf16[64,2048]{1,0:T(8,128)(2,1)} %refs_1_.1), channel_id=1, source_target_pairs={{0,8},{1,9},{2,10},{3,11},{4,12},{5,13},{6,14},{7,15},{8,0},{9,1},... | collective-permute-start | bytes 786440 | tf_op jit(solution)/shard_map/ppermute | solution.py:142
  3.1 0.0 collective-permute-start
  3.1 1.5 %collective-permute-start.15 = (bf16[64,2048]{1,0:T(8,128)(2,1)}, bf16[64,2048]{1,0:T(8,128)(2,1)S(1)}, u32[]{:S(2)}, u32[]{:S(2)}) collective-permute-start(bf16[64,2048]{1,0:T(8,128)(2,1)} %refs_1_.1), channel_id=1, source_target_pairs={{0,4},{1,3},{2,6},{3,1},{4,0},{5,7},{6,2},{7,5},{8,12},{9,11},{10,... | collective-permute-start | bytes 786440 | tf_op jit(solution)/shard_map/ppermute | solution.py:142
  4.7 0.0 collective-permute-done.refs_1_
  4.7 0.3 collective-permute-start.6
  5.0 1.8 %collective-permute-done.14.refs_2_ = bf16[64,2048]{1,0:T(8,128)(2,1)S(1)} collective-permute-done((bf16[64,2048]{1,0:T(8,128)(2,1)}, bf16[64,2048]{1,0:T(8,128)(2,1)S(1)}, u32[]{:S(2)}, u32[]{:S(2)}) %collective-permute-start.14) | collective-permute-done | bytes 262176 | tf_op jit(solution)/shard_map/ppermute | solution.py:142
  6.8 1.6 %collective-permute-start.2 = (bf16[64,2048]{1,0:T(8,128)(2,1)}, bf16[64,2048]{1,0:T(8,128)(2,1)S(1)}, u32[]{:S(2)}, u32[]{:S(2)}) collective-permute-start(bf16[64,2048]{1,0:T(8,128)(2,1)} %refs_1_.1), channel_id=1, source_target_pairs={{0,24},{1,25},{2,26},{3,27},{4,28},{5,29},{6,30},{7,31},{8,16},{9,... | collective-permute-start | bytes 786440 | tf_op jit(solution)/shard_map/ppermute | solution.py:142
  8.4 2.7 %collective-permute-done.10.refs_1_ = bf16[64,2048]{1,0:T(8,128)(2,1)S(1)} collective-permute-done((bf16[64,2048]{1,0:T(8,128)(2,1)}, bf16[64,2048]{1,0:T(8,128)(2,1)S(1)}, u32[]{:S(2)}, u32[]{:S(2)}) %collective-permute-start.10) | collective-permute-done | bytes 262176 | tf_op jit(solution)/shard_map/ppermute | solution.py:142
  11.1 1.0 %collective-permute-start.11 = (bf16[64,2048]{1,0:T(8,128)(2,1)S(1)}, bf16[64,2048]{1,0:T(8,128)(2,1)S(1)}, u32[]{:S(2)}, u32[]{:S(2)}) collective-permute-start(bf16[64,2048]{1,0:T(8,128)(2,1)S(1)} %collective-permute-done.10.refs_1_), channel_id=1, source_target_pairs={{0,2},{1,5},{2,0},{3,7},{4,6},{5,1},{6,4},{7,3},{8,10},{9,13},{10,... | collective-permute-start | bytes 786440 | tf_op jit(solution)/shard_map/ppermute | solution.py:142
  12.1 0.0 collective-permute-done.15.refs_3_
  12.1 0.9 %collective-permute-start.16 = (bf16[64,2048]{1,0:T(8,128)(2,1)S(1)}, bf16[64,2048]{1,0:T(8,128)(2,1)S(1)}, u32[]{:S(2)}, u32[]{:S(2)}) collective-permute-start(bf16[64,2048]{1,0:T(8,128)(2,1)S(1)} %collective-permute-done.14.refs_2_), channel_id=1, source_target_pairs={{0,4},{1,3},{2,6},{3,1},{4,0},{5,7},{6,2},{7,5},{8,12},{9,11},{10,... | collective-permute-start | bytes 786440 | tf_op jit(solution)/shard_map/ppermute | solution.py:142
  13.0 10.3 %collective-permute-done.6.refs_1_ = bf16[64,2048]{1,0:T(8,128)(2,1)S(1)} collective-permute-done((bf16[64,2048]{1,0:T(8,128)(2,1)}, bf16[64,2048]{1,0:T(8,128)(2,1)S(1)}, u32[]{:S(2)}, u32[]{:S(2)}) %collective-permute-start.6) | collective-permute-done | bytes 262176 | tf_op jit(solution)/shard_map/ppermute | solution.py:142
  23.3 1.2 %collective-permute-start.7 = (bf16[64,2048]{1,0:T(8,128)(2,1)S(1)}, bf16[64,2048]{1,0:T(8,128)(2,1)S(1)}, u32[]{:S(2)}, u32[]{:S(2)}) collective-permute-start(bf16[64,2048]{1,0:T(8,128)(2,1)S(1)} %collective-permute-done.6.refs_1_), channel_id=1, source_target_pairs={{0,2},{1,5},{2,0},{3,7},{4,6},{5,1},{6,4},{7,3},{8,10},{9,13},{10,... | collective-permute-start | bytes 786440 | tf_op jit(solution)/shard_map/ppermute | solution.py:142
  24.5 6.3 %collective-permute-done.2.refs_1_ = bf16[64,2048]{1,0:T(8,128)(2,1)S(1)} collective-permute-done((bf16[64,2048]{1,0:T(8,128)(2,1)}, bf16[64,2048]{1,0:T(8,128)(2,1)S(1)}, u32[]{:S(2)}, u32[]{:S(2)}) %collective-permute-start.2) | collective-permute-done | bytes 262176 | tf_op jit(solution)/shard_map/ppermute | solution.py:142
  30.8 1.5 %collective-permute-start.12 = (bf16[64,2048]{1,0:T(8,128)(2,1)S(1)}, bf16[64,2048]{1,0:T(8,128)(2,1)S(1)}, u32[]{:S(2)}, u32[]{:S(2)}) collective-permute-start(bf16[64,2048]{1,0:T(8,128)(2,1)S(1)} %collective-permute-done.10.refs_1_), channel_id=1, source_target_pairs={{0,4},{1,3},{2,6},{3,1},{4,0},{5,7},{6,2},{7,5},{8,12},{9,11},{10,... | collective-permute-start | bytes 786440 | tf_op jit(solution)/shard_map/ppermute | solution.py:142
  32.3 0.0 collective-permute-done.11.refs_2_
  32.3 1.4 %collective-permute-start.3 = (bf16[64,2048]{1,0:T(8,128)(2,1)S(1)}, bf16[64,2048]{1,0:T(8,128)(2,1)S(1)}, u32[]{:S(2)}, u32[]{:S(2)}) collective-permute-start(bf16[64,2048]{1,0:T(8,128)(2,1)S(1)} %collective-permute-done.2.refs_1_), channel_id=1, source_target_pairs={{0,2},{1,5},{2,0},{3,7},{4,6},{5,1},{6,4},{7,3},{8,10},{9,13},{10,... | collective-permute-start | bytes 786440 | tf_op jit(solution)/shard_map/ppermute | solution.py:142
  33.8 0.0 collective-permute-done.1.refs_3_
  33.8 0.6 %collective-permute-start.13 = (bf16[64,2048]{1,0:T(8,128)(2,1)S(1)}, bf16[64,2048]{1,0:T(8,128)(2,1)S(1)}, u32[]{:S(2)}, u32[]{:S(2)}) collective-permute-start(bf16[64,2048]{1,0:T(8,128)(2,1)S(1)} %collective-permute-done.11.refs_2_), channel_id=1, source_target_pairs={{0,4},{1,3},{2,6},{3,1},{4,0},{5,7},{6,2},{7,5},{8,12},{9,11},{10,... | collective-permute-start | bytes 786440 | tf_op jit(solution)/shard_map/ppermute | solution.py:142
  34.4 0.0 copy-start.1
  34.4 0.7 %copy-done.1 = s32[16,4]{0,1:T(4,128)S(1)} copy-done((s32[16,4]{0,1:T(4,128)S(1)}, s32[16,4]{0,1:T(4,128)}, u32[]{:S(2)}) %copy-start.1) | copy-done | bytes 280
  35.1 2.8 %panel.1.refs_0_ = bf16[4,2048,256]{2,1,0:T(8,128)(2,1)S(1)} custom-call(s32[4,16]{1,0:T(4,128)S(1)} %bitcast.2, s32[4,16]{1,0:T(4,128)S(1)} %collective-permute-done.refs_1_, bf16[2048,512]{1,0:T(8,128)(2,1)} %refs_2_.1, bf16[2048,512]{1,0:T(8,128)(2,1)S(1)} %collective-permute-done.1.refs_3_), custom_call_target="tpu_custom_call" | custom-call | bytes 4194304 | tf_op jit(solution)/shard_map/panel/pallas_call | solution.py:61
  37.9 0.0 collective-permute-done.16.refs_4_
  37.9 1.5 %collective-permute-start.8 = (bf16[64,2048]{1,0:T(8,128)(2,1)S(1)}, bf16[64,2048]{1,0:T(8,128)(2,1)S(1)}, u32[]{:S(2)}, u32[]{:S(2)}) collective-permute-start(bf16[64,2048]{1,0:T(8,128)(2,1)S(1)} %collective-permute-done.6.refs_1_), channel_id=1, source_target_pairs={{0,4},{1,3},{2,6},{3,1},{4,0},{5,7},{6,2},{7,5},{8,12},{9,11},{10,... | collective-permute-start | bytes 786440 | tf_op jit(solution)/shard_map/ppermute | solution.py:142
  39.4 0.0 collective-permute-done.7.refs_2_
  39.4 0.6 %collective-permute-start.9 = (bf16[64,2048]{1,0:T(8,128)(2,1)S(1)}, bf16[64,2048]{1,0:T(8,128)(2,1)S(1)}, u32[]{:S(2)}, u32[]{:S(2)}) collective-permute-start(bf16[64,2048]{1,0:T(8,128)(2,1)S(1)} %collective-permute-done.7.refs_2_), channel_id=1, source_target_pairs={{0,4},{1,3},{2,6},{3,1},{4,0},{5,7},{6,2},{7,5},{8,12},{9,11},{10,... | collective-permute-start | bytes 786440 | tf_op jit(solution)/shard_map/ppermute | solution.py:142
  40.0 0.0 copy-done
  40.0 3.0 %shard_map.37.refs_5_ = f32[2048,2048]{1,0:T(8,128)S(1)} custom-call(bf16[4,2048,256]{2,1,0:T(8,128)(2,1)S(1)} %panel.1.refs_0_, bf16[64,2048]{1,0:T(8,128)(2,1)S(1)} %copy-done, bf16[64,2048]{1,0:T(8,128)(2,1)S(1)} %collective-permute-done.14.refs_2_, bf16[64,2048]{1,0:T(8,128)(2,1)S(1)} %collective-permute-done.15.refs_3_, ...), custom_call_target="tpu_custom_call" | custom-call | flops 2147483648 | bytes 8388608 | tf_op jit(solution)/shard_map/pallas_call | solution.py:115
  43.0 0.0 collective-permute-done.12.refs_3_
  43.0 1.5 %collective-permute-start.4 = (bf16[64,2048]{1,0:T(8,128)(2,1)S(1)}, bf16[64,2048]{1,0:T(8,128)(2,1)S(1)}, u32[]{:S(2)}, u32[]{:S(2)}) collective-permute-start(bf16[64,2048]{1,0:T(8,128)(2,1)S(1)} %collective-permute-done.2.refs_1_), channel_id=1, source_target_pairs={{0,4},{1,3},{2,6},{3,1},{4,0},{5,7},{6,2},{7,5},{8,12},{9,11},{10,... | collective-permute-start | bytes 786440 | tf_op jit(solution)/shard_map/ppermute | solution.py:142
  44.5 0.0 collective-permute-done.3.refs_2_
  44.5 0.6 %collective-permute-start.5 = (bf16[64,2048]{1,0:T(8,128)(2,1)S(1)}, bf16[64,2048]{1,0:T(8,128)(2,1)S(1)}, u32[]{:S(2)}, u32[]{:S(2)}) collective-permute-start(bf16[64,2048]{1,0:T(8,128)(2,1)S(1)} %collective-permute-done.3.refs_2_), channel_id=1, source_target_pairs={{0,4},{1,3},{2,6},{3,1},{4,0},{5,7},{6,2},{7,5},{8,12},{9,11},{10,... | collective-permute-start | bytes 786440 | tf_op jit(solution)/shard_map/ppermute | solution.py:142
  45.1 0.0 collective-permute-done.13.refs_4_
  45.1 4.5 %shard_map.38.refs_5_ = f32[2048,2048]{1,0:T(8,128)S(1)} custom-call(bf16[4,2048,256]{2,1,0:T(8,128)(2,1)S(1)} %panel.1.refs_0_, bf16[64,2048]{1,0:T(8,128)(2,1)S(1)} %collective-permute-done.10.refs_1_, bf16[64,2048]{1,0:T(8,128)(2,1)S(1)} %collective-permute-done.11.refs_2_, ...), custom_call_target="tpu_custom_call", output_to_operand_aliasing={{}: (5, {})} | custom-call | flops 2147483648 | bytes 8388608 | tf_op jit(solution)/shard_map/pallas_call | solution.py:115
  49.6 0.0 collective-permute-done.8.refs_3_
  49.6 0.0 collective-permute-done.9.refs_4_
  49.6 4.5 %shard_map.39.refs_5_ = f32[2048,2048]{1,0:T(8,128)S(1)} custom-call(bf16[4,2048,256]{2,1,0:T(8,128)(2,1)S(1)} %panel.1.refs_0_, bf16[64,2048]{1,0:T(8,128)(2,1)S(1)} %collective-permute-done.6.refs_1_, bf16[64,2048]{1,0:T(8,128)(2,1)S(1)} %collective-permute-done.7.refs_2_, ...), custom_call_target="tpu_custom_call", output_to_operand_aliasing={{}: (5, {})} | custom-call | flops 2147483648 | bytes 8388608 | tf_op jit(solution)/shard_map/pallas_call | solution.py:115
  54.1 0.0 collective-permute-done.4.refs_3_
  54.1 0.0 collective-permute-done.5.refs_4_
  54.1 4.9 %shard_map.40 = bf16[2048,2048]{1,0:T(8,128)(2,1)} custom-call(bf16[4,2048,256]{2,1,0:T(8,128)(2,1)S(1)} %panel.1.refs_0_, bf16[64,2048]{1,0:T(8,128)(2,1)S(1)} %collective-permute-done.2.refs_1_, bf16[64,2048]{1,0:T(8,128)(2,1)S(1)} %collective-permute-done.3.refs_2_, bf16[64,2048]{1,0:T(8,128)(2,1)S(1)} %collective-permute-done.4.refs_3_, ...), custom_call_target="tpu_custom_call" | custom-call | flops 2147483648 | bytes 8388608 | tf_op jit(solution)/shard_map/pallas_call | solution.py:115
Async XLA Ops:
  0.0 40.0 %copy-start = (bf16[64,2048]{1,0:T(8,128)(2,1)S(1)}, bf16[64,2048]{1,0:T(8,128)(2,1)}, u32[]{:S(2)}) copy-start(bf16[64,2048]{1,0:T(8,128)(2,1)} %refs_1_.1) | copy-start | bytes 786436
  0.0 33.8 %collective-permute-start.1 = (bf16[2048,512]{1,0:T(8,128)(2,1)}, bf16[2048,512]{1,0:T(8,128)(2,1)S(1)}, u32[]{:S(2)}, u32[]{:S(2)}) collective-permute-start(bf16[2048,512]{1,0:T(8,128)(2,1)} %refs_2_.1), channel_id=1, source_target_pairs={{0,1},{1,0},{2,3},{3,2},{4,5},{5,4},{6,7},{7,6},{8,9},{9,8},{10,11... | collective-permute-start | bytes 6291464 | tf_op jit(solution)/shard_map/ppermute | solution.py:145
  0.0 6.8 %collective-permute-start.14 = (bf16[64,2048]{1,0:T(8,128)(2,1)}, bf16[64,2048]{1,0:T(8,128)(2,1)S(1)}, u32[]{:S(2)}, u32[]{:S(2)}) collective-permute-start(bf16[64,2048]{1,0:T(8,128)(2,1)} %refs_1_.1), channel_id=1, source_target_pairs={{0,2},{1,5},{2,0},{3,7},{4,6},{5,1},{6,4},{7,3},{8,10},{9,13},{10,... | collective-permute-start | bytes 786440 | tf_op jit(solution)/shard_map/ppermute | solution.py:142
  1.6 9.5 %collective-permute-start.10 = (bf16[64,2048]{1,0:T(8,128)(2,1)}, bf16[64,2048]{1,0:T(8,128)(2,1)S(1)}, u32[]{:S(2)}, u32[]{:S(2)}) collective-permute-start(bf16[64,2048]{1,0:T(8,128)(2,1)} %refs_1_.1), channel_id=1, source_target_pairs={{0,8},{1,9},{2,10},{3,11},{4,12},{5,13},{6,14},{7,15},{8,0},{9,1},... | collective-permute-start | bytes 786440 | tf_op jit(solution)/shard_map/ppermute | solution.py:142
  3.1 1.5 %collective-permute-start = (s32[4,16]{1,0:T(4,128)}, s32[4,16]{1,0:T(4,128)S(1)}, u32[]{:S(2)}, u32[]{:S(2)}) collective-permute-start(s32[4,16]{1,0:T(4,128)} %bitcast.1), channel_id=1, source_target_pairs={{0,1},{1,0},{2,3},{3,2},{4,5},{5,4},{6,7},{7,6},{8,9},{9,8},{10,11... | collective-permute-start | bytes 776 | tf_op jit(solution)/shard_map/ppermute | solution.py:145
  3.1 9.0 %collective-permute-start.15 = (bf16[64,2048]{1,0:T(8,128)(2,1)}, bf16[64,2048]{1,0:T(8,128)(2,1)S(1)}, u32[]{:S(2)}, u32[]{:S(2)}) collective-permute-start(bf16[64,2048]{1,0:T(8,128)(2,1)} %refs_1_.1), channel_id=1, source_target_pairs={{0,4},{1,3},{2,6},{3,1},{4,0},{5,7},{6,2},{7,5},{8,12},{9,11},{10,... | collective-permute-start | bytes 786440 | tf_op jit(solution)/shard_map/ppermute | solution.py:142
  4.7 18.6 %collective-permute-start.6 = (bf16[64,2048]{1,0:T(8,128)(2,1)}, bf16[64,2048]{1,0:T(8,128)(2,1)S(1)}, u32[]{:S(2)}, u32[]{:S(2)}) collective-permute-start(bf16[64,2048]{1,0:T(8,128)(2,1)} %refs_1_.1), channel_id=1, source_target_pairs={{0,16},{1,17},{2,18},{3,19},{4,20},{5,21},{6,22},{7,23},{8,24},{9,... | collective-permute-start | bytes 786440 | tf_op jit(solution)/shard_map/ppermute | solution.py:142
  6.8 24.0 %collective-permute-start.2 = (bf16[64,2048]{1,0:T(8,128)(2,1)}, bf16[64,2048]{1,0:T(8,128)(2,1)S(1)}, u32[]{:S(2)}, u32[]{:S(2)}) collective-permute-start(bf16[64,2048]{1,0:T(8,128)(2,1)} %refs_1_.1), channel_id=1, source_target_pairs={{0,24},{1,25},{2,26},{3,27},{4,28},{5,29},{6,30},{7,31},{8,16},{9,... | collective-permute-start | bytes 786440 | tf_op jit(solution)/shard_map/ppermute | solution.py:142
  11.1 21.2 %collective-permute-start.11 = (bf16[64,2048]{1,0:T(8,128)(2,1)S(1)}, bf16[64,2048]{1,0:T(8,128)(2,1)S(1)}, u32[]{:S(2)}, u32[]{:S(2)}) collective-permute-start(bf16[64,2048]{1,0:T(8,128)(2,1)S(1)} %collective-permute-done.10.refs_1_), channel_id=1, source_target_pairs={{0,2},{1,5},{2,0},{3,7},{4,6},{5,1},{6,4},{7,3},{8,10},{9,13},{10,... | collective-permute-start | bytes 786440 | tf_op jit(solution)/shard_map/ppermute | solution.py:142
  12.1 25.8 %collective-permute-start.16 = (bf16[64,2048]{1,0:T(8,128)(2,1)S(1)}, bf16[64,2048]{1,0:T(8,128)(2,1)S(1)}, u32[]{:S(2)}, u32[]{:S(2)}) collective-permute-start(bf16[64,2048]{1,0:T(8,128)(2,1)S(1)} %collective-permute-done.14.refs_2_), channel_id=1, source_target_pairs={{0,4},{1,3},{2,6},{3,1},{4,0},{5,7},{6,2},{7,5},{8,12},{9,11},{10,... | collective-permute-start | bytes 786440 | tf_op jit(solution)/shard_map/ppermute | solution.py:142
  23.3 16.1 %collective-permute-start.7 = (bf16[64,2048]{1,0:T(8,128)(2,1)S(1)}, bf16[64,2048]{1,0:T(8,128)(2,1)S(1)}, u32[]{:S(2)}, u32[]{:S(2)}) collective-permute-start(bf16[64,2048]{1,0:T(8,128)(2,1)S(1)} %collective-permute-done.6.refs_1_), channel_id=1, source_target_pairs={{0,2},{1,5},{2,0},{3,7},{4,6},{5,1},{6,4},{7,3},{8,10},{9,13},{10,... | collective-permute-start | bytes 786440 | tf_op jit(solution)/shard_map/ppermute | solution.py:142
  30.8 12.2 %collective-permute-start.12 = (bf16[64,2048]{1,0:T(8,128)(2,1)S(1)}, bf16[64,2048]{1,0:T(8,128)(2,1)S(1)}, u32[]{:S(2)}, u32[]{:S(2)}) collective-permute-start(bf16[64,2048]{1,0:T(8,128)(2,1)S(1)} %collective-permute-done.10.refs_1_), channel_id=1, source_target_pairs={{0,4},{1,3},{2,6},{3,1},{4,0},{5,7},{6,2},{7,5},{8,12},{9,11},{10,... | collective-permute-start | bytes 786440 | tf_op jit(solution)/shard_map/ppermute | solution.py:142
  32.3 12.2 %collective-permute-start.3 = (bf16[64,2048]{1,0:T(8,128)(2,1)S(1)}, bf16[64,2048]{1,0:T(8,128)(2,1)S(1)}, u32[]{:S(2)}, u32[]{:S(2)}) collective-permute-start(bf16[64,2048]{1,0:T(8,128)(2,1)S(1)} %collective-permute-done.2.refs_1_), channel_id=1, source_target_pairs={{0,2},{1,5},{2,0},{3,7},{4,6},{5,1},{6,4},{7,3},{8,10},{9,13},{10,... | collective-permute-start | bytes 786440 | tf_op jit(solution)/shard_map/ppermute | solution.py:142
  33.8 11.3 %collective-permute-start.13 = (bf16[64,2048]{1,0:T(8,128)(2,1)S(1)}, bf16[64,2048]{1,0:T(8,128)(2,1)S(1)}, u32[]{:S(2)}, u32[]{:S(2)}) collective-permute-start(bf16[64,2048]{1,0:T(8,128)(2,1)S(1)} %collective-permute-done.11.refs_2_), channel_id=1, source_target_pairs={{0,4},{1,3},{2,6},{3,1},{4,0},{5,7},{6,2},{7,5},{8,12},{9,11},{10,... | collective-permute-start | bytes 786440 | tf_op jit(solution)/shard_map/ppermute | solution.py:142
  34.4 0.7 %copy-start.1 = (s32[16,4]{0,1:T(4,128)S(1)}, s32[16,4]{0,1:T(4,128)}, u32[]{:S(2)}) copy-start(s32[16,4]{0,1:T(4,128)} %param.4) | copy-start | bytes 772
  37.9 11.7 %collective-permute-start.8 = (bf16[64,2048]{1,0:T(8,128)(2,1)S(1)}, bf16[64,2048]{1,0:T(8,128)(2,1)S(1)}, u32[]{:S(2)}, u32[]{:S(2)}) collective-permute-start(bf16[64,2048]{1,0:T(8,128)(2,1)S(1)} %collective-permute-done.6.refs_1_), channel_id=1, source_target_pairs={{0,4},{1,3},{2,6},{3,1},{4,0},{5,7},{6,2},{7,5},{8,12},{9,11},{10,... | collective-permute-start | bytes 786440 | tf_op jit(solution)/shard_map/ppermute | solution.py:142
  39.4 10.2 %collective-permute-start.9 = (bf16[64,2048]{1,0:T(8,128)(2,1)S(1)}, bf16[64,2048]{1,0:T(8,128)(2,1)S(1)}, u32[]{:S(2)}, u32[]{:S(2)}) collective-permute-start(bf16[64,2048]{1,0:T(8,128)(2,1)S(1)} %collective-permute-done.7.refs_2_), channel_id=1, source_target_pairs={{0,4},{1,3},{2,6},{3,1},{4,0},{5,7},{6,2},{7,5},{8,12},{9,11},{10,... | collective-permute-start | bytes 786440 | tf_op jit(solution)/shard_map/ppermute | solution.py:142
  43.0 11.1 %collective-permute-start.4 = (bf16[64,2048]{1,0:T(8,128)(2,1)S(1)}, bf16[64,2048]{1,0:T(8,128)(2,1)S(1)}, u32[]{:S(2)}, u32[]{:S(2)}) collective-permute-start(bf16[64,2048]{1,0:T(8,128)(2,1)S(1)} %collective-permute-done.2.refs_1_), channel_id=1, source_target_pairs={{0,4},{1,3},{2,6},{3,1},{4,0},{5,7},{6,2},{7,5},{8,12},{9,11},{10,... | collective-permute-start | bytes 786440 | tf_op jit(solution)/shard_map/ppermute | solution.py:142
  44.5 9.6 %collective-permute-start.5 = (bf16[64,2048]{1,0:T(8,128)(2,1)S(1)}, bf16[64,2048]{1,0:T(8,128)(2,1)S(1)}, u32[]{:S(2)}, u32[]{:S(2)}) collective-permute-start(bf16[64,2048]{1,0:T(8,128)(2,1)S(1)} %collective-permute-done.3.refs_2_), channel_id=1, source_target_pairs={{0,4},{1,3},{2,6},{3,1},{4,0},{5,7},{6,2},{7,5},{8,12},{9,11},{10,... | collective-permute-start | bytes 786440 | tf_op jit(solution)/shard_map/ppermute | solution.py:142
